TPU v7x, 512 devices: a whole 4x4x16 slice. The times are simulated.
512 devices in a mesh: blk: 16 (over y, x_hi, core), group: 32 (over x_lo, z).
Axes of the slice: x: 4 (x_hi: 2, x_lo: 2; x = x_hi * 2 + x_lo), y: 4, z: 16, core: 2. Of those that a mesh axis runs over, the one named last changes fastest.
Arguments:
- student_features: bfloat16 [65536, 768], P(('blk', 'group')), may hold values from -8 to 8
- teacher_image: bfloat16 [65536, 1152], P(('blk', 'group')), may hold values from -8 to 8
- text_embeds: bfloat16 [65536, 1152], P(('blk', 'group')), may hold values from -8 to 8
- pair_ids: int32 [65536], replicated, may hold values from 0 to 8191
- head_weights: bfloat16 [1152, 768], replicated, may hold values from -1 to 1
- moment_first: float32 [1152, 768], P('group'), may hold values from -4 to 4
- moment_second: float32 [1152, 768], P('group'), may hold values from 0.01 to 0.3
Outputs:
- row_loss: float32 [65536], P(('blk', 'group'))
- new_first: float32 [1152, 768], P('group')
- new_second: float32 [1152, 768], P('group')
- new_weights: bfloat16 [1152, 768], replicated
All inputs are finite; a program needn't handle non-finite values.
Results may differ from a plain program's by a relative error of at most 0.0025.
The roundings to bfloat16 on the way count: a program that leaves them out, or rounds other values in their place, can miss the bound.
Values may be sent and summed in bfloat16 or wider, within the bound.
No kernel may reach another device: no remote copies, remote signals or barrier semaphores. Data moves between devices by JAX's collectives and lax.ppermute only.
A program may use at most 64 MiB of HBM per device.

v0:
```python
import jax
import jax.numpy as jnp
from jax import lax
from jax.sharding import PartitionSpec as P

student_scale = 20.0
student_bias = -1.0
teacher_scale = 25.0
teacher_bias = -1.5
label_mix = 0.5
norm_eps = 1e-06
beta_one = 0.9
beta_two = 0.95
learn_rate = 0.01
weight_decay = 0.0001
adam_eps = 1e-08
adam_step = 100.0


def from_partner(shard, axis, bit):
    return lax.ppermute(shard, axis, [(i, i ^ 1 << bit) for i in range(lax.axis_size(axis))])


def unit_rows(values):
    values = values.astype(jnp.float32)
    return values * lax.rsqrt(jnp.sum(values * values, axis=-1, keepdims=True) + norm_eps)


def pair_terms(student_rows, teacher_rows, left_ids, text_rows, right_ids):
    dims = (((1,), (1,)), ((), ()))
    student_logit = (
        student_scale
        * lax.dot_general(student_rows, text_rows, dims, preferred_element_type=jnp.float32)
        + student_bias
    )
    teacher_logit = (
        teacher_scale
        * lax.dot_general(teacher_rows, text_rows, dims, preferred_element_type=jnp.float32)
        + teacher_bias
    )
    labels = (left_ids[:, None] == right_ids[None, :]).astype(jnp.float32)
    target = (1.0 - label_mix) * labels + label_mix * jax.nn.sigmoid(teacher_logit)
    losses = jnp.sum(jax.nn.softplus(student_logit) - target * student_logit, axis=1)
    coeff = (jax.nn.sigmoid(student_logit) - target).astype(jnp.bfloat16)
    pulled = jnp.dot(coeff, text_rows, preferred_element_type=jnp.float32)
    return (losses, pulled)


def per_device(
    student_features,
    teacher_image,
    text_embeds,
    pair_ids,
    head_weights,
    moment_first,
    moment_second,
):
    row_count = student_features.shape[0]
    blk_count = lax.axis_size("blk")
    group_count = lax.axis_size("group")
    swap_bit = group_count.bit_length() - 2
    group_index = lax.axis_index("group")
    partner_index = (group_index + group_count // 2) % group_count
    blk_index = lax.axis_index("blk")
    projected = lax.dot_general(
        student_features, head_weights, (((1,), (1,)), ((), ())), preferred_element_type=jnp.float32
    )
    inverse = lax.rsqrt(jnp.sum(projected * projected, axis=-1, keepdims=True) + norm_eps)
    student = projected * inverse
    student_b = student.astype(jnp.bfloat16)
    teacher_b = unit_rows(teacher_image).astype(jnp.bfloat16)
    texts_b = unit_rows(text_embeds).astype(jnp.bfloat16)
    ids_grid = pair_ids.reshape(blk_count, group_count, row_count)
    own_ids = lax.dynamic_index_in_dim(ids_grid, group_index, 1, keepdims=False)
    far_ids = lax.dynamic_index_in_dim(ids_grid, partner_index, 1, keepdims=False)
    left_ids = lax.dynamic_index_in_dim(own_ids, blk_index, 0, keepdims=False)
    far_block = from_partner(texts_b, "group", swap_bit)
    paired = jnp.concatenate([texts_b, far_block], axis=0)
    paired_ids = jnp.stack([own_ids, far_ids], axis=1).reshape(-1)
    losses, pulled = pair_terms(
        student_b,
        teacher_b,
        left_ids,
        lax.all_gather(paired, "blk", axis=0, tiled=True),
        paired_ids,
    )
    totals = (losses, pulled)
    losses, pulled = totals
    row_loss = losses / row_count
    grad_student = student_scale / row_count * pulled
    grad_projected = (
        inverse * (grad_student - student * jnp.sum(student * grad_student, axis=-1, keepdims=True))
    ).astype(jnp.bfloat16)
    shard_rows = moment_first.shape[0]
    group_grad = lax.psum_scatter(
        lax.dot_general(
            grad_projected,
            student_features,
            (((0,), (0,)), ((), ())),
            preferred_element_type=jnp.float32,
        ),
        "group",
        scatter_dimension=0,
        tiled=True,
    )
    head_grad = lax.psum(group_grad, "blk")
    new_first = beta_one * moment_first + (1.0 - beta_one) * head_grad
    new_second = beta_two * moment_second + (1.0 - beta_two) * head_grad * head_grad
    first_hat = new_first / (1.0 - beta_one**adam_step)
    second_hat = new_second / (1.0 - beta_two**adam_step)
    own_weights = lax.dynamic_slice_in_dim(
        head_weights, group_index * shard_rows, shard_rows, 0
    ).astype(jnp.float32)
    updated = own_weights - learn_rate * (
        first_hat / (jnp.sqrt(second_hat) + adam_eps) + weight_decay * own_weights
    )
    new_weights = lax.all_gather(updated.astype(jnp.bfloat16), "group", axis=0, tiled=True)
    return (row_loss, new_first, new_second, new_weights)


def solution(mesh):
    placed = (
        P(("blk", "group"), None),
        P(("blk", "group"), None),
        P(("blk", "group"), None),
        P(),
        P(),
        P("group", None),
        P("group", None),
    )
    return jax.shard_map(
        per_device,
        mesh=mesh,
        in_specs=placed,
        out_specs=(P(("blk", "group")), P("group", None), P("group", None), P()),
        check_vma=False,
    )
```

profile of v0, /device:TPU:8, one launch (start us, length us, event | category | flops | bytes accessed | tf_op | source)
XLA Modules:
  0.0 531.9 jit_solution(12891333635255561007)
XLA Ops:
  7.2 1.3 fusion.12
  8.5 1.1 fusion.13
  9.6 3.4 collective-permute-start
  13.0 7.2 %collective-permute-done = bf16[128,1152]{1,0:T(8,128)(2,1)S(1)} collective-permute-done((bf16[128,1152]{1,0:T(8,128)(2,1)S(1)}, bf16[128,1152]{1,0:T(8,128)(2,1)S(1)}, u32[]{:S(2)}, u32[]{:S(2)}) %collective-permute-start) | collective-permute-done | bytes 294944 | tf_op jit(solution)/shard_map/ppermute | solution.py:21
  20.2 0.9 pad_maximum_fusion
  21.2 0.7 fusion.27
  21.9 0.9 constant_dynamic-slice_fusion.2
  23.0 0.8 multiply_reduce_fusion.1
  23.8 93.0 %all-gather.4.cloned.1.call-done = bf16[4096,1152]{1,0:T(8,128)(2,1)} async-done(((bf16[256,1152]{1,0:T(8,128)(2,1)}), bf16[4096,1152]{1,0:T(8,128)(2,1)}) %all-gather.4.cloned.1.call-update) | async-done | bytes 9437200 | tf_op jit(solution)/shard_map/all_gather | solution.py:84
  116.8 7.1 %fusion.8 = f32[128,4096]{1,0:T(8,128)S(1)} fusion(bf16[4096,1152]{1,0:T(8,128)(2,1)} %all-gather.4.cloned.1.call-done, s32[4096]{0:T(1024)S(1)} %bitcast.15, s32[128]{0:T(128)S(1)} %fusion.27, bf16[128,1152]{1,0:T(8,128)(2,1)S(1)} %copy-done.2, f32[128]{0:T(128)S(1)} %add_rsqrt_fusion), kind=kOutput, calls=%fused_computation.10 | convolution fusion | flops 1213120512 | bytes 11846656 | tf_op jit(solution)/shard_map/dot_general | solution.py:38
  123.8 3.8 fusion.10
  127.7 1.9 multiply_reduce_fusion
  129.5 2.5 fusion.16
  132.1 82.5 %fusion = f32[40,768]{1,0:T(8,128)S(1)} fusion(f32[1152,768]{1,0:T(8,128)} %fusion.16), kind=kCustom, calls=%all-reduce-scatter | all-reduce-scatter fusion | flops 983041 | bytes 3663872
  214.6 4.1 collective-permute-start.3
  218.7 1.5 collective-permute-start.2
  220.2 2.9 collective-permute-start.1
  223.1 5.6 %collective-permute-start.4 = (f32[4,768]{1,0:T(4,128)S(1)}, f32[4,768]{1,0:T(4,128)S(1)}, u32[]{:S(2)}, u32[]{:S(2)}) collective-permute-start(f32[4,768]{1,0:T(4,128)S(1)} %slice), channel_id=1, source_target_pairs={{0,4},{1,5},{2,6},{3,7},{4,8},{5,9},{6,10},{7,11},{8,12},{9,13},{1... | collective-permute-start | bytes 36872
  228.7 1.3 dynamic-slice.6
  231.3 0.7 constant_dynamic-slice_fusion
  232.1 149.7 %all-reduce.4.cloned.1.call-done = f32[36,768]{1,0:T(8,128)} async-done(((f32[36,768]{1,0:T(8,128)}), f32[36,768]{1,0:T(8,128)}) %all-reduce.4.cloned.1.call-update) | async-done | bytes 110608 | tf_op jit(solution)/shard_map/psum | solution.py:106
  381.7 1.7 fusion.26
  384.0 137.8 %all-gather.6.cloned.1.call-done = bf16[32,36,768]{2,1,0:T(8,128)(2,1)} async-done(((bf16[1,36,768]{2,1,0:T(8,128)(2,1)}), bf16[32,36,768]{2,1,0:T(8,128)(2,1)}) %all-gather.6.cloned.1.call-update) | async-done | bytes 1769488 | tf_op jit(solution)/shard_map/all_gather | solution.py:117
  521.8 3.6 reshape.37
  (30 shorter events, 1.5 us)
Async XLA Ops:
  7.2 15.8 %copy-start = (bf16[128,768]{1,0:T(8,128)(2,1)S(1)}, bf16[128,768]{1,0:T(8,128)(2,1)}, u32[]{:S(2)}) copy-start(bf16[128,768]{1,0:T(8,128)(2,1)} %param.7) | copy-start | bytes 589828
  7.2 15.6 %copy-start.2 = (bf16[128,1152]{1,0:T(8,128)(2,1)S(1)}, bf16[128,1152]{1,0:T(8,128)(2,1)}, u32[]{:S(2)}) copy-start(bf16[128,1152]{1,0:T(8,128)(2,1)} %param.8) | copy-start | bytes 884740
  7.2 15.8 %copy-start.1 = (bf16[1152,768]{1,0:T(8,128)(2,1)S(1)}, bf16[1152,768]{1,0:T(8,128)(2,1)}, u32[]{:S(2)}) copy-start(bf16[1152,768]{1,0:T(8,128)(2,1)} %param.11) | copy-start | bytes 5308420
  7.2 109.6 %all-gather.4.cloned.1.call-start = ((), (), s32[]{:S(2)}) async-start(), calls=%async_computation | async-start | bytes 10027008 | tf_op jit(solution)/shard_map/all_gather | solution.py:84
  9.6 10.6 %collective-permute-start = (bf16[128,1152]{1,0:T(8,128)(2,1)S(1)}, bf16[128,1152]{1,0:T(8,128)(2,1)S(1)}, u32[]{:S(2)}, u32[]{:S(2)}) collective-permute-start(bf16[128,1152]{1,0:T(8,128)(2,1)S(1)} %fusion.13), channel_id=1, source_target_pairs={{0,16},{1,17},{2,18},{3,19},{4,20},{5,21},{6,22},{7,23},{8,24},{9,... | collective-permute-start | bytes 884744 | tf_op jit(solution)/shard_map/ppermute | solution.py:21
  21.1 360.6 %all-reduce.4.cloned.1.call-start = ((), (), s32[]{:S(2)}) async-start(), calls=%async_computation.1 | async-start | bytes 245760 | tf_op jit(solution)/shard_map/psum | solution.py:106
  116.8 7.1 %copy-start.5 = (bf16[4096,1152]{1,0:T(8,128)(2,1)S(1)}, bf16[4096,1152]{1,0:T(8,128)(2,1)}, u32[]{:S(2)}) copy-start(bf16[4096,1152]{1,0:T(8,128)(2,1)} %all-gather.4.cloned.1.call-done) | copy-start | bytes 28311556
  132.1 249.7 %copy-start.3 = (f32[36,768]{1,0:T(8,128)S(1)}, f32[36,768]{1,0:T(8,128)}, u32[]{:S(2)}) copy-start(f32[36,768]{1,0:T(8,128)} %param.13) | copy-start | bytes 331780
  132.1 249.7 %copy-start.4 = (f32[36,768]{1,0:T(8,128)S(1)}, f32[36,768]{1,0:T(8,128)}, u32[]{:S(2)}) copy-start(f32[36,768]{1,0:T(8,128)} %param.12) | copy-start | bytes 331780
  214.6 16.1 %collective-permute-start.3 = (f32[40,768]{1,0:T(8,128)S(1)}, f32[40,768]{1,0:T(8,128)S(1)}, u32[]{:S(2)}, u32[]{:S(2)}) collective-permute-start(f32[40,768]{1,0:T(8,128)S(1)} %fusion), channel_id=1, source_target_pairs={{0,3},{1,4},{2,5},{3,6},{4,7},{5,8},{6,9},{7,10},{8,11},{9,12},{10... | collective-permute-start | bytes 368648
  218.7 12.0 %collective-permute-start.2 = (f32[40,768]{1,0:T(8,128)S(1)}, f32[40,768]{1,0:T(8,128)S(1)}, u32[]{:S(2)}, u32[]{:S(2)}) collective-permute-start(f32[40,768]{1,0:T(8,128)S(1)} %fusion), channel_id=1, source_target_pairs={{0,2},{1,3},{2,4},{3,5},{4,6},{5,7},{6,8},{7,9},{8,10},{9,11},{10,... | collective-permute-start | bytes 368648
  220.2 10.5 %collective-permute-start.1 = (f32[40,768]{1,0:T(8,128)S(1)}, f32[40,768]{1,0:T(8,128)S(1)}, u32[]{:S(2)}, u32[]{:S(2)}) collective-permute-start(f32[40,768]{1,0:T(8,128)S(1)} %fusion), channel_id=1, source_target_pairs={{0,1},{1,2},{2,3},{3,4},{4,5},{5,6},{6,7},{7,8},{8,9},{9,10},{10,1... | collective-permute-start | bytes 368648
  223.1 7.5 %collective-permute-start.4 = (f32[4,768]{1,0:T(4,128)S(1)}, f32[4,768]{1,0:T(4,128)S(1)}, u32[]{:S(2)}, u32[]{:S(2)}) collective-permute-start(f32[4,768]{1,0:T(4,128)S(1)} %slice), channel_id=1, source_target_pairs={{0,4},{1,5},{2,6},{3,7},{4,8},{5,9},{6,10},{7,11},{8,12},{9,13},{1... | collective-permute-start | bytes 36872
  232.0 289.8 %all-gather.6.cloned.1.call-start = ((), (), s32[]{:S(2)}) async-start(), calls=%async_computation.2 | async-start | bytes 2027520 | tf_op jit(solution)/shard_map/all_gather | solution.py:117
Sparse Core Ops, SparseCore 0:
  21.2 95.4 all-gather.3
  232.1 149.5 all-reduce.3
  384.4 137.3 all-gather.5
where the time goes:
time: 532 us
  waiting for transfers between devices  388 us (73%)
  blocking collectives  82.5 us (16%)
  starting transfers between devices  17.6 us (3%)
  matrix products  16.1 us (3%)
  between operations  14.6 us (3%)
  local copies, waits for them, and re-layouts  7.8 us (1%)
  other arithmetic  5.56 us (1%)
    psum x1, waiting for transfers between devices, per_device(): head_grad = lax.psum(group_grad, 'blk')  150 us
    all_gather x1, waiting for transfers between devices, per_device(): lax.all_gather(updated.astype(jnp.bfloat16), 'group', axis=0, tiled=True)  138 us
    all_gather x1, waiting for transfers between devices, per_device(): lax.all_gather(paired, 'blk', axis=0, tiled=True)  93 us
    unnamed x1, blocking collectives  82.5 us
    unnamed x4, starting transfers between devices  14.1 us
  transfers between devices with their start and end apart: 8, of which 4 were waited for; matrix products, arithmetic and copies ran while one was open for 1% of the time, Pallas kernels for 0%

commit v1 on v0

--- a/solution.py
+++ b/solution.py
@@ -15,6 +15,12 @@
 weight_decay = 0.0001
 adam_eps = 1e-08
 adam_step = 100.0
+
+
+def gather_and_add(value, name):
+    parts = lax.all_gather(value, name, axis=0, tiled=False)
+    total = parts.sum(axis=0)
+    return total
 
 
 def from_partner(shard, axis, bit):
@@ -103,7 +109,7 @@
         scatter_dimension=0,
         tiled=True,
     )
-    head_grad = lax.psum(group_grad, "blk")
+    head_grad = gather_and_add(group_grad, "blk")
     new_first = beta_one * moment_first + (1.0 - beta_one) * head_grad
     new_second = beta_two * moment_second + (1.0 - beta_two) * head_grad * head_grad
     first_hat = new_first / (1.0 - beta_one**adam_step)

time: 532 us -> 442 us (0.83)
  waiting for transfers between devices: 388 us -> 296 us
    psum x1 -> x0, waiting for transfers between devices: 150 us -> none  [per_device(): head_grad = lax.psum(group_grad, 'blk')]
    all_gather x0 -> x1, waiting for transfers between devices: none -> 63.9 us  [gather_and_add(): parts = lax.all_gather(value, name, axis=0, tiled=False)]
    all_gather x1, waiting for transfers between devices: 138 us -> 132 us  [per_device(): lax.all_gather(updated.astype(jnp.bfloat16), 'group', axis=0, tiled=True)]
where the time goes in v1:
time: 442 us; the launch traced here: 441 us
  waiting for transfers between devices  296 us (67%)
  blocking collectives  82.5 us (19%)
  starting transfers between devices  17.8 us (4%)
  matrix products  16.1 us (4%)
  between operations  14.6 us (3%)
  local copies, waits for them, and re-layouts  7.81 us (2%)
  other arithmetic  6.32 us (1%)
    all_gather x1, waiting for transfers between devices, per_device(): lax.all_gather(updated.astype(jnp.bfloat16), 'group', axis=0, tiled=True)  132 us
    all_gather x1, waiting for transfers between devices, per_device(): lax.all_gather(paired, 'blk', axis=0, tiled=True)  93 us
    unnamed x1, blocking collectives  82.5 us
    all_gather x1, waiting for transfers between devices, gather_and_add(): parts = lax.all_gather(value, name, axis=0, tiled=False)  63.9 us
    unnamed x4, starting transfers between devices  14.3 us
  transfers between devices with their start and end apart: 8, of which 4 were waited for; matrix products, arithmetic and copies ran while one was open for 1% of the time, Pallas kernels for 0%

profile of v1, /device:TPU:8, one launch (start us, length us, event | category | flops | bytes accessed | tf_op | source)
XLA Modules:
  0.0 441.5 jit_solution(6610632112047682264)
XLA Ops:
  7.2 1.3 fusion.12
  8.5 1.1 fusion.13
  9.6 3.4 collective-permute-start
  13.0 7.2 %collective-permute-done = bf16[128,1152]{1,0:T(8,128)(2,1)S(1)} collective-permute-done((bf16[128,1152]{1,0:T(8,128)(2,1)S(1)}, bf16[128,1152]{1,0:T(8,128)(2,1)S(1)}, u32[]{:S(2)}, u32[]{:S(2)}) %collective-permute-start) | collective-permute-done | bytes 294944 | tf_op jit(solution)/shard_map/ppermute | solution.py:27
  20.2 0.9 pad_maximum_fusion
  21.2 0.7 fusion.27
  21.9 0.9 constant_dynamic-slice_fusion.1
  23.0 0.8 multiply_reduce_fusion.1
  23.8 93.0 %all-gather.7.cloned.1.call-done = bf16[4096,1152]{1,0:T(8,128)(2,1)} async-done(((bf16[256,1152]{1,0:T(8,128)(2,1)}), bf16[4096,1152]{1,0:T(8,128)(2,1)}) %all-gather.7.cloned.1.call-update) | async-done | bytes 9437200 | tf_op jit(solution)/shard_map/all_gather | solution.py:90
  116.8 7.1 %fusion.8 = f32[128,4096]{1,0:T(8,128)S(1)} fusion(bf16[4096,1152]{1,0:T(8,128)(2,1)} %all-gather.7.cloned.1.call-done, s32[4096]{0:T(1024)S(1)} %bitcast.17, s32[128]{0:T(128)S(1)} %fusion.27, bf16[128,1152]{1,0:T(8,128)(2,1)S(1)} %copy-done.2, f32[128]{0:T(128)S(1)} %add_rsqrt_fusion), kind=kOutput, calls=%fused_computation.10 | convolution fusion | flops 1213120512 | bytes 11846656 | tf_op jit(solution)/shard_map/dot_general | solution.py:44
  123.8 3.8 fusion.10
  127.7 1.9 multiply_reduce_fusion
  129.5 2.5 fusion.16
  132.1 82.5 %fusion = f32[40,768]{1,0:T(8,128)S(1)} fusion(f32[1152,768]{1,0:T(8,128)} %fusion.16), kind=kCustom, calls=%all-reduce-scatter | all-reduce-scatter fusion | flops 983041 | bytes 3663872
  214.6 4.2 collective-permute-start.3
  218.8 2.0 collective-permute-start.2
  220.8 2.4 collective-permute-start.1
  223.2 5.7 %collective-permute-start.4 = (f32[4,768]{1,0:T(4,128)S(1)}, f32[4,768]{1,0:T(4,128)S(1)}, u32[]{:S(2)}, u32[]{:S(2)}) collective-permute-start(f32[4,768]{1,0:T(4,128)S(1)} %slice), channel_id=1, source_target_pairs={{0,4},{1,5},{2,6},{3,7},{4,8},{5,9},{6,10},{7,11},{8,12},{9,13},{1... | collective-permute-start | bytes 36872
  228.9 1.3 dynamic-slice.6
  232.2 63.9 %all-gather.9.cloned.1.call-done = f32[16,36,768]{2,1,0:T(8,128)} async-done(((f32[1,36,768]{2,1,0:T(8,128)}), f32[16,36,768]{2,1,0:T(8,128)}) %all-gather.9.cloned.1.call-update) | async-done | bytes 1769488 | tf_op jit(solution)/shard_map/all_gather | solution.py:21
  296.1 1.6 reduce_sum.59
  297.8 0.8 fusion.26
  299.1 132.2 %all-gather.11.cloned.1.call-done = bf16[32,36,768]{2,1,0:T(8,128)(2,1)} async-done(((bf16[1,36,768]{2,1,0:T(8,128)(2,1)}), bf16[32,36,768]{2,1,0:T(8,128)(2,1)}) %all-gather.11.cloned.1.call-update) | async-done | bytes 1769488 | tf_op jit(solution)/shard_map/all_gather | solution.py:123
  431.3 3.6 reshape.40
  (31 shorter events, 2.2 us)
Async XLA Ops:
  7.2 15.8 %copy-start = (bf16[128,768]{1,0:T(8,128)(2,1)S(1)}, bf16[128,768]{1,0:T(8,128)(2,1)}, u32[]{:S(2)}) copy-start(bf16[128,768]{1,0:T(8,128)(2,1)} %param.7) | copy-start | bytes 589828
  7.2 15.6 %copy-start.2 = (bf16[128,1152]{1,0:T(8,128)(2,1)S(1)}, bf16[128,1152]{1,0:T(8,128)(2,1)}, u32[]{:S(2)}) copy-start(bf16[128,1152]{1,0:T(8,128)(2,1)} %param.8) | copy-start | bytes 884740
  7.2 15.8 %copy-start.1 = (bf16[1152,768]{1,0:T(8,128)(2,1)S(1)}, bf16[1152,768]{1,0:T(8,128)(2,1)}, u32[]{:S(2)}) copy-start(bf16[1152,768]{1,0:T(8,128)(2,1)} %param.11) | copy-start | bytes 5308420
  7.2 109.6 %all-gather.7.cloned.1.call-start = ((), (), s32[]{:S(2)}) async-start(), calls=%async_computation | async-start | bytes 10027008 | tf_op jit(solution)/shard_map/all_gather | solution.py:90
  9.6 10.6 %collective-permute-start = (bf16[128,1152]{1,0:T(8,128)(2,1)S(1)}, bf16[128,1152]{1,0:T(8,128)(2,1)S(1)}, u32[]{:S(2)}, u32[]{:S(2)}) collective-permute-start(bf16[128,1152]{1,0:T(8,128)(2,1)S(1)} %fusion.13), channel_id=1, source_target_pairs={{0,16},{1,17},{2,18},{3,19},{4,20},{5,21},{6,22},{7,23},{8,24},{9,... | collective-permute-start | bytes 884744 | tf_op jit(solution)/shard_map/ppermute | solution.py:27
  21.1 275.0 %all-gather.9.cloned.1.call-start = ((), (), s32[]{:S(2)}) async-start(), calls=%async_computation.1 | async-start | bytes 2088960 | tf_op jit(solution)/shard_map/all_gather | solution.py:21
  116.8 7.1 %copy-start.5 = (bf16[4096,1152]{1,0:T(8,128)(2,1)S(1)}, bf16[4096,1152]{1,0:T(8,128)(2,1)}, u32[]{:S(2)}) copy-start(bf16[4096,1152]{1,0:T(8,128)(2,1)} %all-gather.7.cloned.1.call-done) | copy-start | bytes 28311556
  214.5 83.3 %copy-start.3 = (f32[36,768]{1,0:T(8,128)S(1)}, f32[36,768]{1,0:T(8,128)}, u32[]{:S(2)}) copy-start(f32[36,768]{1,0:T(8,128)} %param.13) | copy-start | bytes 331780
  214.6 83.2 %copy-start.4 = (f32[36,768]{1,0:T(8,128)S(1)}, f32[36,768]{1,0:T(8,128)}, u32[]{:S(2)}) copy-start(f32[36,768]{1,0:T(8,128)} %param.12) | copy-start | bytes 331780
  214.6 16.3 %collective-permute-start.3 = (f32[40,768]{1,0:T(8,128)S(1)}, f32[40,768]{1,0:T(8,128)S(1)}, u32[]{:S(2)}, u32[]{:S(2)}) collective-permute-start(f32[40,768]{1,0:T(8,128)S(1)} %fusion), channel_id=1, source_target_pairs={{0,3},{1,4},{2,5},{3,6},{4,7},{5,8},{6,9},{7,10},{8,11},{9,12},{10... | collective-permute-start | bytes 368648
  218.8 12.1 %collective-permute-start.2 = (f32[40,768]{1,0:T(8,128)S(1)}, f32[40,768]{1,0:T(8,128)S(1)}, u32[]{:S(2)}, u32[]{:S(2)}) collective-permute-start(f32[40,768]{1,0:T(8,128)S(1)} %fusion), channel_id=1, source_target_pairs={{0,2},{1,3},{2,4},{3,5},{4,6},{5,7},{6,8},{7,9},{8,10},{9,11},{10,... | collective-permute-start | bytes 368648
  220.8 10.1 %collective-permute-start.1 = (f32[40,768]{1,0:T(8,128)S(1)}, f32[40,768]{1,0:T(8,128)S(1)}, u32[]{:S(2)}, u32[]{:S(2)}) collective-permute-start(f32[40,768]{1,0:T(8,128)S(1)} %fusion), channel_id=1, source_target_pairs={{0,1},{1,2},{2,3},{3,4},{4,5},{5,6},{6,7},{7,8},{8,9},{9,10},{10,1... | collective-permute-start | bytes 368648
  223.2 7.6 %collective-permute-start.4 = (f32[4,768]{1,0:T(4,128)S(1)}, f32[4,768]{1,0:T(4,128)S(1)}, u32[]{:S(2)}, u32[]{:S(2)}) collective-permute-start(f32[4,768]{1,0:T(4,128)S(1)} %slice), channel_id=1, source_target_pairs={{0,4},{1,5},{2,6},{3,7},{4,8},{5,9},{6,10},{7,11},{8,12},{9,13},{1... | collective-permute-start | bytes 36872
  232.2 199.1 %all-gather.11.cloned.1.call-start = ((), (), s32[]{:S(2)}) async-start(), calls=%async_computation.2 | async-start | bytes 2027520 | tf_op jit(solution)/shard_map/all_gather | solution.py:123
Sparse Core Ops, SparseCore 0:
  21.2 95.4 all-gather.6
  232.3 63.7 all-gather.8
  298.8 132.4 all-gather.10
